TPU v7x, 32 devices: a whole 2x2x4 slice. The times are simulated.
32 devices in a mesh: row: 4 (over z), col: 8 (over y, x, core).
Axes of the slice: x: 2, y: 2, z: 4, core: 2. Of those that a mesh axis runs over, the one named last changes fastest.
Arguments:
- activations: bfloat16 [4096, 8192], P('row', 'col'), may hold values from -6 to 6
- errors: bfloat16 [4096, 8192], P('row', 'col'), may hold values from -6 to 6
- act_proj: bfloat16 [8192, 128], P('col'), may hold values from -0.0625 to 0.0625
- err_proj: bfloat16 [8192, 128], P('col'), may hold values from -0.0625 to 0.0625
- lengths: int32 [4, 64], P('row'), may hold values from 1 to 256, 1024 in all within a row
- ridge: float32 [16384, 16384], P('row', 'col'), may hold values from -4 to 36, as said below
- pivot_inverse: float32 [2, 512, 512], replicated, may hold values from -1 to 1
Outputs:
- eliminated: float32 [16384, 16384], P('row', 'col')
Inputs may be any that keep to these rules, and one draw needn't show every extreme that they name: The lengths of one row group sum to 1024. `ridge`: Symmetric.
All inputs are finite; a program needn't handle non-finite values.
Results may differ from a plain program's by a relative error of at most 0.0074.
Values may be sent and summed in bfloat16 or wider, within the bound.
No kernel may reach another device: no remote copies, remote signals or barrier semaphores. Data moves between devices by JAX's collectives and lax.ppermute only.
A program may use at most 192 MiB of HBM per device.

v0:
```python
import jax
import jax.numpy as jnp
from jax import lax
from jax.sharding import PartitionSpec as P


def spread_2(array, axis, root):
    mine = lax.axis_index(axis) == root
    return lax.psum(jnp.where(mine, array, jnp.zeros_like(array)), axis)


def as_sent(array):

    def short(part):
        return part.astype(jnp.bfloat16) if part.dtype == jnp.float32 else part

    return jax.tree.map(short, array)


def per_device(activations, errors, act_proj, err_proj, lengths, ridge, pivot_inverse):
    part_act = jnp.dot(activations, act_proj, preferred_element_type=jnp.float32)
    part_err = jnp.dot(errors, err_proj, preferred_element_type=jnp.float32)
    summed_act, summed_err = lax.psum((part_act, part_err), "col")
    proj_act = summed_act.astype(jnp.bfloat16)
    col_count = lax.axis_size("col")
    row_count = lax.axis_size("row")
    col_ratio = col_count // row_count
    col_idx = lax.axis_index("col")
    row_idx = lax.axis_index("row")
    proj_width = act_proj.shape[1]
    err_share = proj_width // col_count
    err_part = lax.dynamic_slice_in_dim(summed_err, col_idx * err_share, err_share, 1).astype(
        jnp.bfloat16
    )
    lengths_row = lengths[0]
    captions_dev = lengths_row.shape[0]
    tokens_dev = activations.shape[0]
    caption_end = jnp.cumsum(lengths_row)
    caption_start = caption_end - lengths_row
    positions = jnp.arange(tokens_dev, dtype=jnp.int32)[:, None]
    member = ((positions >= caption_start[None, :]) & (positions < caption_end[None, :])).astype(
        jnp.bfloat16
    )
    weighted = (member[:, :, None] * err_part[:, None, :]).reshape(
        tokens_dev, captions_dev * err_share
    )
    local_grads = lax.dot_general(
        weighted, proj_act, (((0,), (0,)), ((), ())), preferred_element_type=jnp.float32
    )
    local_grads = local_grads.reshape(captions_dev, err_share * proj_width).astype(jnp.bfloat16)
    col_grads = lax.all_gather(local_grads, "row", axis=0, tiled=True)
    row_parts = []
    for column_step in range(col_ratio):
        row_parts.append(spread_2(col_grads, "col", row_idx * col_ratio + column_step))
    row_grads = jnp.concatenate(row_parts, axis=1)
    captions_all = col_grads.shape[0]
    gram_tile = lax.dot_general(
        row_grads, col_grads, (((0,), (0,)), ((), ())), preferred_element_type=jnp.float32
    )
    matrix = ridge + gram_tile / captions_all
    tile_rows, tile_cols = ridge.shape
    row_start = row_idx * tile_rows
    col_start = col_idx * tile_cols
    row_ids = row_start + jnp.arange(tile_rows, dtype=jnp.int32)
    col_ids = col_start + jnp.arange(tile_cols, dtype=jnp.int32)
    panel_width = pivot_inverse.shape[1]

    def apply_inverse(columns, start_col, inverse):
        result = jnp.dot(columns, inverse.T, precision=lax.Precision.HIGHEST)
        return jnp.where(row_ids[:, None] >= start_col, result, 0.0)

    first_panel = apply_inverse(matrix[:, 0:panel_width], 0, pivot_inverse[0])
    pivot_block = spread_2(
        first_panel[panel_width : 2 * panel_width].astype(jnp.bfloat16), "row", 0
    ).astype(jnp.float32)
    lower_first = jnp.where(row_ids[:, None] >= panel_width, first_panel, 0.0)
    second_block = matrix[:, panel_width : 2 * panel_width] - jnp.dot(
        lower_first, pivot_block.T, precision=lax.Precision.HIGHEST
    )
    second_panel = apply_inverse(second_block, panel_width, pivot_inverse[1])
    both_panels = jnp.concatenate([first_panel, second_panel], axis=1)
    row_panel = spread_2(as_sent(both_panels), "col", 0).astype(both_panels.dtype)
    col_piece = lax.dynamic_slice_in_dim(row_panel, col_idx % col_ratio * tile_cols, tile_cols, 0)
    col_panel = spread_2(as_sent(col_piece), "row", col_idx // col_ratio).astype(col_piece.dtype)
    row_panel, col_panel = (row_panel, col_panel)
    current = matrix
    stop_col = 2 * panel_width
    lower_part = jnp.where(row_ids[:, None] >= stop_col, row_panel, 0.0)
    upper_part = jnp.where(col_ids[:, None] >= stop_col, col_panel, 0.0)
    current = current - jnp.dot(lower_part, upper_part.T, precision=lax.Precision.HIGHEST)
    offset = jnp.clip(0 - col_start, 0, tile_cols - (stop_col - 0))
    placed = lax.dynamic_update_slice(jnp.zeros_like(current), row_panel, (jnp.int32(0), offset))
    in_panel = (col_ids >= 0) & (col_ids < stop_col)
    current = jnp.where(in_panel[None, :], placed, current)
    above_panel = ((row_ids >= 0) & (row_ids < stop_col))[:, None] & (col_ids >= stop_col)[None, :]
    return jnp.where(above_panel, 0.0, current)


def solution(mesh):
    in_specs = (
        P("row", "col"),
        P("row", "col"),
        P("col", None),
        P("col", None),
        P("row", None),
        P("row", "col"),
        P(),
    )
    out_specs = P("row", "col")
    return jax.shard_map(
        per_device, mesh=mesh, in_specs=in_specs, out_specs=out_specs, check_vma=False
    )
```

profile of v0, /device:TPU:0, one launch (start us, length us, event | category | flops | bytes accessed | tf_op | source)
XLA Modules:
  0.0 710.1 jit_solution(3458219125566349725)
XLA Ops:
  6.5 1.6 copy-done
  8.1 1.8 fusion.41
  9.9 2.3 fusion.42
  13.9 52.8 %all-reduce.15 = (bf16[1024,128]{0,1:T(8,128)(2,1)S(1)}, bf16[1024,128]{1,0:T(8,128)(2,1)S(1)}) all-reduce(f32[1024,128]{0,1:T(8,128)S(1)} %fusion.41, f32[1024,128]{1,0:T(8,128)S(1)} %fusion.42), channel_id=1, replica_groups=mesh['row'=4,'col'=8] {'col'}, use_global_device_ids=true, to_apply=%region_1.0 | all-reduce | flops 262144 | bytes 1572864 | tf_op jit(solution)/shard_map/psum | solution.py:23
  67.7 0.8 convert_element_type.35
  68.6 27.7 %all-gather.2.cloned.1.call-done = bf16[256,2048]{1,0:T(8,128)(2,1)} async-done(((bf16[64,2048]{1,0:T(8,128)(2,1)}), bf16[256,2048]{1,0:T(8,128)(2,1)}) %all-gather.2.cloned.1.call-update) | async-done | bytes 1048592 | tf_op jit(solution)/shard_map/all_gather | solution.py:51
  96.3 2.7 broadcast_select_fusion.1
  99.0 61.7 %all-reduce.14.cloned.1.call-done = (bf16[256,2048]{1,0:T(8,128)(2,1)}, bf16[256,2048]{1,0:T(8,128)(2,1)}) async-done(((bf16[256,2048]{1,0:T(8,128)(2,1)}, bf16[256,2048]{1,0:T(8,128)(2,1)}), (bf16[256,2048]{1,0:T(8,128)(2,1)}, bf16[256,2048]{1,0:T(8,128)(2,1)})) %all-reduce.14.cloned.1.call-update) | async-done | bytes 2097168 | tf_op jit(solution)/shard_map/psum | solution.py:9
  160.8 25.6 %multiply_add_fusion = f32[4096,2048]{1,0:T(8,128)} fusion(f32[4096,2048]{1,0:T(8,128)} %param.12, bf16[256,2048]{1,0:T(8,128)(2,1)} %all-gather.2.cloned.1.call-done, bf16[256,2048]{1,0:T(8,128)(2,1)} %get-tuple-element.7, bf16[256,2048]{1,0:T(8,128)(2,1)} %get-tuple-element.8), kind=kOutput, calls=%fused_computation.1 | convolution fusion | flops 4315938816 | bytes 70254592 | tf_op jit(solution)/shard_map/dot_general | solution.py:57
  186.4 18.0 %select_convert_fusion.1 = (bf16[4096,512]{1,0:T(8,128)(2,1)S(1)}, f32[4096,512]{1,0:T(8,128)}) fusion(pred[4096]{0:T(1024)(128)(4,1)S(1)} %fusion.31, f32[2,512,512]{2,1,0:T(8,128)S(1)} %copy-done.4, f32[4096,2048]{1,0:T(8,128)} %multiply_add_fusion), kind=kOutput, calls=%fused_computation.17 | convolution fusion | flops 12886999040 | bytes 22024192 | tf_op jit(solution)/shard_map/dot_general | solution.py:69
  204.4 2.0 copy-done.2
  206.5 0.9 slice_select_fusion
  207.6 37.6 %all-reduce.8.cloned.1.call-done = bf16[512,512]{1,0:T(8,128)(2,1)} async-done(((bf16[512,512]{1,0:T(8,128)(2,1)}), bf16[512,512]{1,0:T(8,128)(2,1)}) %all-reduce.8.cloned.1.call-update) | async-done | bytes 524304 | tf_op jit(solution)/shard_map/psum | solution.py:9
  245.2 9.5 %fusion.7 = f32[4096,512]{1,0:T(8,128)S(1)} fusion(bf16[512,512]{1,0:T(8,128)(2,1)} %all-reduce.8.cloned.1.call-done, f32[4096,512]{1,0:T(8,128)} %get-tuple-element.12, pred[4096]{0:T(1024)(128)(4,1)S(1)} %fusion.29, pred[4096]{0:T(1024)(128)(4,1)S(1)} %fusion.31), kind=kOutput, calls=%fused_computation.13 | convolution fusion | flops 12889096192 | bytes 17309696 | tf_op jit(solution)/shard_map/dot_general | solution.py:77
  254.7 16.7 %select_convert_fusion = bf16[4096,512]{1,0:T(8,128)(2,1)S(1)} fusion(f32[4096,512]{1,0:T(8,128)S(1)} %fusion.7, f32[4096,2048]{1,0:T(8,128)} %multiply_add_fusion, pred[4096]{0:T(1024)(128)(4,1)S(1)} %fusion.29, f32[2,512,512]{2,1,0:T(8,128)S(1)} %copy-done.4), kind=kOutput, calls=%fused_computation.12 | convolution fusion | flops 12891193344 | bytes 22024192 | tf_op jit(solution)/shard_map/dot_general | solution.py:69
  271.4 4.3 maximum_select_fusion
  276.1 125.9 %all-reduce.10.cloned.1.call-done = bf16[4096,1024]{1,0:T(8,128)(2,1)} async-done(((bf16[4096,1024]{1,0:T(8,128)(2,1)}), bf16[4096,1024]{1,0:T(8,128)(2,1)}) %all-reduce.10.cloned.1.call-update) | async-done | bytes 8388624 | tf_op jit(solution)/shard_map/psum | solution.py:9
  401.9 11.2 %convert_element_type.36 = f32[4096,1024]{1,0:T(8,128)} convert(bf16[4096,1024]{1,0:T(8,128)(2,1)} %all-reduce.10.cloned.1.call-done) | non-fusion elementwise | flops 4194304 | bytes 25165824 | tf_op jit(solution)/shard_map/convert_element_type | solution.py:82
  413.2 6.6 fusion.11
  419.8 11.5 %broadcast_in_dim.81 = f32[4096,2048]{1,0:T(8,128)} broadcast(f32[]{:T(128)} %constant.29.clone.1), dimensions={} | broadcast | bytes 33554436 | tf_op jit(solution)/shard_map/jit(_where)/broadcast_in_dim | solution.py:96
  431.4 78.0 %dynamic_update_slice.3 = f32[4096,2048]{1,0:T(8,128)} dynamic-update-slice(f32[4096,2048]{1,0:T(8,128)} %broadcast_in_dim.81, f32[4096,1024]{1,0:T(8,128)} %convert_element_type.36, s32[]{:T(128)} %constant.24.clone.1, s32[]{:T(128)S(6)} %min.4) | dynamic-update-slice | bytes 33554436 | tf_op jit(solution)/shard_map/dynamic_update_slice | solution.py:92
  509.4 65.7 %all-reduce.12.cloned.1.call-done = bf16[2048,1024]{1,0:T(8,128)(2,1)} async-done(((bf16[2048,1024]{1,0:T(8,128)(2,1)}), bf16[2048,1024]{1,0:T(8,128)(2,1)}) %all-reduce.12.cloned.1.call-update) | async-done | bytes 4194320 | tf_op jit(solution)/shard_map/psum | solution.py:9
  575.0 5.2 fusion.57
  580.2 123.4 %select_select_fusion = f32[4096,2048]{1,0:T(8,128)} fusion(f32[4096,2048]{1,0:T(8,128)} %dynamic_update_slice.3, f32[4096,2048]{1,0:T(8,128)} %multiply_add_fusion, pred[2048]{0:T(1024)(128)(4,1)S(1)} %get-tuple-element.16, pred[2048]{0:T(1024)(128)(4,1)S(1)} %get-tuple-element.15, pred[4096]{0:T(1024)(128)(4,1)S(1)} %get-tuple-element.14, ...), kind=kOutput, calls=%fused_computation | convolution fusion | flops 103121158144 | bytes 117452800 | tf_op jit(solution)/shard_map/dot_general | solution.py:90
  (30 shorter events, 3.3 us)
Async XLA Ops:
  6.5 1.6 copy-start
  6.5 89.7 %all-gather.2.cloned.1.call-start = ((), (), s32[]{:S(2)}) async-start(), calls=%async_computation | async-start | bytes 1310720 | tf_op jit(solution)/shard_map/all_gather | solution.py:51
  68.5 92.2 %all-reduce.14.cloned.1.call-start = ((), (), s32[]{:S(2)}) async-start(), calls=%async_computation.4 | async-start | bytes 4194304 | tf_op jit(solution)/shard_map/psum | solution.py:9
  99.0 146.3 %all-reduce.8.cloned.1.call-start = ((), (), s32[]{:S(2)}) async-start(), calls=%async_computation.1 | async-start | bytes 1048576 | tf_op jit(solution)/shard_map/psum | solution.py:9
  160.8 25.6 %copy-start.4 = (f32[2,512,512]{2,1,0:T(8,128)S(1)}, f32[2,512,512]{2,1,0:T(8,128)}, u32[]{:S(2)}) copy-start(f32[2,512,512]{2,1,0:T(8,128)} %param.13) | copy-start | bytes 6291460
  204.4 2.0 copy-start.2
  207.4 194.6 %all-reduce.10.cloned.1.call-start = ((), (), s32[]{:S(2)}) async-start(), calls=%async_computation.2 | async-start | bytes 16777216 | tf_op jit(solution)/shard_map/psum | solution.py:9
  254.7 16.7 %copy-start.3 = (bf16[4096,512]{1,0:T(8,128)(2,1)S(1)}, bf16[4096,512]{1,0:T(8,128)(2,1)}, u32[]{:S(2)}) copy-start(bf16[4096,512]{1,0:T(8,128)(2,1)} %copy-done.2) | copy-start | bytes 12582916
  275.8 299.3 %all-reduce.12.cloned.1.call-start = ((), (), s32[]{:S(2)}) async-start(), calls=%async_computation.3 | async-start | bytes 8388608 | tf_op jit(solution)/shard_map/psum | solution.py:9
  580.2 123.4 %copy-start.1 = (bf16[1024,1024]{1,0:T(8,128)(2,1)S(1)}, bf16[1024,1024]{1,0:T(8,128)(2,1)}, u32[]{:S(2)}) copy-start(bf16[1024,1024]{1,0:T(8,128)(2,1)} %param.8) | copy-start | bytes 6291460
Sparse Core Ops, SparseCore 0:
  68.7 27.5 all-gather.1
  99.5 61.1 all-reduce.13
  207.5 37.6 all-reduce.7
  275.9 125.9 all-reduce.9
  419.9 155.1 all-reduce.11
where the time goes:
time: 712 us; the launch traced here: 710 us
  waiting for transfers between devices  319 us (45%)
  matrix products  198 us (28%)
  local copies, waits for them, and re-layouts  94.8 us (13%)
  blocking collectives  52.8 us (7%)
  other arithmetic  32 us (4%)
  between operations  13.3 us (2%)
    psum x4, waiting for transfers between devices, spread_2(): return lax.psum(jnp.where(mine, array, jnp.zeros_like(array)), axis)  291 us
    dot_general x1, matrix products, per_device(): jnp.dot(lower_part, upper_part.T, precision=lax.Precision.HIGHEST)  123 us
    dynamic_update_slice x1, local copies, waits for them, and re-layouts, per_device(): lax.dynamic_update_slice(jnp.zeros_like(current), row_panel, (jnp.int32(0...  78 us
    psum x1, blocking collectives, per_device(): summed_act, summed_err = lax.psum((part_act, part_err), 'col')  52.8 us
    dot_general x2, matrix products, apply_inverse(): result = jnp.dot(columns, inverse.T, precision=lax.Precision.HIGHEST)  34.7 us
    all_gather x1, waiting for transfers between devices, per_device(): col_grads = lax.all_gather(local_grads, 'row', axis=0, tiled=True)  27.7 us
    dot_general x1, matrix products, per_device(): lax.dot_general(row_grads, col_grads, (((0,), (0,)), ((), ())), preferred...  25.6 us
    select_n x4, other arithmetic, spread_2(): return lax.psum(jnp.where(mine, array, jnp.zeros_like(array)), axis)  14.4 us
  transfers between devices with their start and end apart: 5, of which 5 were waited for; matrix products, arithmetic and copies ran while one was open for 13% of the time, Pallas kernels for 0%

commit v1 on v0

--- a/solution.py
+++ b/solution.py
@@ -6,7 +6,9 @@
 
 def spread_2(array, axis, root):
     mine = lax.axis_index(axis) == root
-    return lax.psum(jnp.where(mine, array, jnp.zeros_like(array)), axis)
+    return jnp.sum(
+        lax.all_gather(jnp.where(mine, array, jnp.zeros_like(array)), axis_name=axis), axis=0
+    )
 
 
 def as_sent(array):

time: 712 us -> 1140 us (1.60)
  waiting for transfers between devices: 319 us -> 674 us
  other arithmetic: 32 us -> 84 us
  local copies, waits for them, and re-layouts: 94.8 us -> 112 us
    all_gather x0 -> x5, waiting for transfers between devices: none -> 646 us  [spread_2(): lax.all_gather(jnp.where(mine, array, jnp.zeros_like(array)), axis_name=a...]
    psum x4 -> x0, waiting for transfers between devices: 291 us -> none  [spread_2(): return lax.psum(jnp.where(mine, array, jnp.zeros_like(array)), axis)]
    reduce_sum x0 -> x5, other arithmetic: none -> 51.5 us  [spread_2(): jnp.sum(lax.all_gather(jnp.where(mine, array, jnp.zeros_like(array)), axi...]
    select_n x0 -> x1, local copies, waits for them, and re-layouts: none -> 12 us  [spread_2(): jnp.where(mine, array, jnp.zeros_like(array))]
  transfers between devices with their start and end apart: 5 -> 6, of which waited for: 5 -> 6; matrix products, arithmetic and copies ran while one was open for 13% -> 9% of each run, Pallas kernels for 0% -> 0%
where the time goes in v1:
time: 1140 us; the launch traced here: 1130 us
  waiting for transfers between devices  674 us (59%)
  matrix products  197 us (17%)
  local copies, waits for them, and re-layouts  112 us (10%)
  other arithmetic  84 us (7%)
  blocking collectives  52.8 us (5%)
  between operations  13.9 us (1%)
    all_gather x5, waiting for transfers between devices, spread_2(): lax.all_gather(jnp.where(mine, array, jnp.zeros_like(array)), axis_name=a...  646 us
    dot_general x1, matrix products, per_device(): jnp.dot(lower_part, upper_part.T, precision=lax.Precision.HIGHEST)  124 us
    dynamic_update_slice x1, local copies, waits for them, and re-layouts, per_device(): lax.dynamic_update_slice(jnp.zeros_like(current), row_panel, (jnp.int32(0...  78.1 us
    psum x1, blocking collectives, per_device(): summed_act, summed_err = lax.psum((part_act, part_err), 'col')  52.8 us
    reduce_sum x5, other arithmetic, spread_2(): jnp.sum(lax.all_gather(jnp.where(mine, array, jnp.zeros_like(array)), axi...  51.5 us
    dot_general x2, matrix products, apply_inverse(): result = jnp.dot(columns, inverse.T, precision=lax.Precision.HIGHEST)  34 us
    all_gather x1, waiting for transfers between devices, per_device(): col_grads = lax.all_gather(local_grads, 'row', axis=0, tiled=True)  27.7 us
    dot_general x1, matrix products, per_device(): lax.dot_general(row_grads, col_grads, (((0,), (0,)), ((), ())), preferred...  24.9 us
  transfers between devices with their start and end apart: 6, of which 6 were waited for; matrix products, arithmetic and copies ran while one was open for 9% of the time, Pallas kernels for 0%

profile of v1, /device:TPU:0, one launch (start us, length us, event | category | flops | bytes accessed | tf_op | source)
XLA Modules:
  0.0 1134.5 jit_solution(2922848804791710989)
XLA Ops:
  13.9 52.8 %all-reduce.2 = (bf16[1024,128]{0,1:T(8,128)(2,1)S(1)}, bf16[1024,128]{1,0:T(8,128)(2,1)S(1)}) all-reduce(f32[1024,128]{0,1:T(8,128)S(1)} %fusion.42, f32[1024,128]{1,0:T(8,128)S(1)} %fusion.43), channel_id=1, replica_groups=mesh['row'=4,'col'=8] {'col'}, use_global_device_ids=true, to_apply=%region_1.0 | all-reduce | flops 262144 | bytes 1572864 | tf_op jit(solution)/shard_map/psum | solution.py:25
  68.6 27.7 %all-gather.11.cloned.1.call-done = bf16[256,2048]{1,0:T(8,128)(2,1)} async-done(((bf16[64,2048]{1,0:T(8,128)(2,1)}), bf16[256,2048]{1,0:T(8,128)(2,1)}) %all-gather.11.cloned.1.call-update) | async-done | bytes 1048592 | tf_op jit(solution)/shard_map/all_gather | solution.py:53
  100.1 52.7 %all-gather.15.cloned.1.call-done = bf16[2048,2048]{1,0:T(8,128)(2,1)} async-done(((bf16[256,2048]{1,0:T(8,128)(2,1)}), bf16[2048,2048]{1,0:T(8,128)(2,1)}) %all-gather.15.cloned.1.call-update) | async-done | bytes 8388624 | tf_op jit(solution)/shard_map/all_gather | solution.py:10
  152.8 5.3 reduce_sum.60
  158.1 50.9 %all-gather.17.cloned.1.call-done = bf16[2048,2048]{1,0:T(8,128)(2,1)} async-done(((bf16[256,2048]{1,0:T(8,128)(2,1)}), bf16[2048,2048]{1,0:T(8,128)(2,1)}) %all-gather.17.cloned.1.call-update) | async-done | bytes 8388624 | tf_op jit(solution)/shard_map/all_gather | solution.py:10
  209.0 5.2 reduce_sum.61
  214.2 24.9 %multiply_add_fusion = f32[4096,2048]{1,0:T(8,128)} fusion(f32[4096,2048]{1,0:T(8,128)} %param.12, bf16[256,2048]{1,0:T(8,128)(2,1)S(1)} %copy-done.4, bf16[256,2048]{1,0:T(8,128)(2,1)S(1)} %reduce_sum.61, bf16[256,2048]{1,0:T(8,128)(2,1)S(1)} %reduce_sum.60), kind=kOutput, calls=%fused_computation.1 | convolution fusion | flops 4315938816 | bytes 70254592 | tf_op jit(solution)/shard_map/dot_general | solution.py:59
  239.1 17.2 %select_convert_fusion.1 = (bf16[4096,512]{0,1:T(8,128)(2,1)S(1)}, f32[4096,512]{0,1:T(8,128)}) fusion(pred[4096]{0:T(1024)(128)(4,1)S(1)} %fusion.32, f32[2,512,512]{2,1,0:T(8,128)} %param.13, f32[4096,2048]{1,0:T(8,128)} %multiply_add_fusion), kind=kOutput, calls=%fused_computation.17 | convolution fusion | flops 12886999040 | bytes 22024192 | tf_op jit(solution)/shard_map/dot_general | solution.py:71
  259.6 45.4 %all-gather.19.cloned.1.call-done = bf16[2048,512]{0,1:T(8,128)(2,1)} async-done(((bf16[512,512]{0,1:T(8,128)(2,1)}), bf16[2048,512]{0,1:T(8,128)(2,1)}) %all-gather.19.cloned.1.call-update) | async-done | bytes 2097168 | tf_op jit(solution)/shard_map/all_gather | solution.py:10
  305.0 3.3 reshape.130
  311.1 9.4 fusion.7
  320.6 16.8 %fusion.11 = bf16[1,4096,512]{1,2,0:T(8,128)(2,1)S(1)} fusion(f32[4096,512]{1,0:T(8,128)S(1)} %fusion.7, f32[4096,2048]{1,0:T(8,128)} %multiply_add_fusion, pred[4096]{0:T(1024)(128)(4,1)S(1)} %fusion.30, f32[2,512,512]{2,1,0:T(8,128)S(1)} %copy-done.5), kind=kOutput, calls=%fused_computation.18 | convolution fusion | flops 12891193344 | bytes 22024192 | tf_op jit(solution)/shard_map/dot_general | solution.py:71
  337.4 4.6 maximum_select_fusion
  341.9 12.0 %copy.12 = bf16[1,4096,1024]{2,1,0:T(8,128)(2,1)} copy(bf16[1,4096,1024]{1,2,0:T(8,128)(2,1)} %maximum_select_fusion) | data formatting | bytes 16777216 | tf_op jit(solution)/shard_map/jit(_where)/select_n | solution.py:10
  354.0 301.6 %all-gather.13.cloned.1.call-done = bf16[8,4096,1024]{2,1,0:T(8,128)(2,1)} async-done(((bf16[1,4096,1024]{2,1,0:T(8,128)(2,1)}), bf16[8,4096,1024]{2,1,0:T(8,128)(2,1)}) %all-gather.13.cloned.1.call-update) | async-done | bytes 67108880 | tf_op jit(solution)/shard_map/all_gather | solution.py:10
  655.6 26.2 %reduce_sum.63 = bf16[4096,1024]{1,0:T(8,128)(2,1)} reduce(bf16[8,4096,1024]{2,1,0:T(8,128)(2,1)} %all-gather.13.cloned.1.call-done, bf16[]{:T(256)} %constant.68.clone.1), dimensions={0}, to_apply=%region_6.7 | reduce | flops 29360128 | bytes 75497472 | tf_op jit(solution)/shard_map/reduce_sum | solution.py:9
  681.8 11.3 convert_element_type.53
  693.0 6.7 fusion.12
  699.8 13.5 %broadcast_in_dim.81 = f32[4096,2048]{1,0:T(8,128)} broadcast(f32[]{:T(128)} %constant.64.clone.1), dimensions={} | broadcast | bytes 33554436 | tf_op jit(solution)/shard_map/jit(_where)/broadcast_in_dim | solution.py:98
  713.2 78.1 %dynamic_update_slice.3 = f32[4096,2048]{1,0:T(8,128)} dynamic-update-slice(f32[4096,2048]{1,0:T(8,128)} %broadcast_in_dim.81, f32[4096,1024]{1,0:T(8,128)} %convert_element_type.53, s32[]{:T(128)} %constant.32.clone.1, s32[]{:T(128)S(6)} %min.4) | dynamic-update-slice | bytes 33554436 | tf_op jit(solution)/shard_map/dynamic_update_slice | solution.py:94
  791.3 195.3 %all-gather.21.cloned.1.call-done = bf16[8192,1024]{1,0:T(8,128)(2,1)} async-done(((bf16[2048,1024]{1,0:T(8,128)(2,1)}), bf16[8192,1024]{1,0:T(8,128)(2,1)}) %all-gather.21.cloned.1.call-update) | async-done | bytes 16777232 | tf_op jit(solution)/shard_map/all_gather | solution.py:10
  986.6 12.0 %reduce_sum.64 = bf16[2048,1024]{1,0:T(8,128)(2,1)} reduce(bf16[4,2048,1024]{2,1,0:T(8,128)(2,1)} %bitcast.34, bf16[]{:T(256)} %constant.68.clone.1), dimensions={0}, to_apply=%region_7.8 | reduce | flops 6291456 | bytes 20971522 | tf_op jit(solution)/shard_map/reduce_sum | solution.py:9
  998.7 5.2 fusion.58
  1003.9 123.6 %select_select_fusion = f32[4096,2048]{1,0:T(8,128)} fusion(f32[4096,2048]{1,0:T(8,128)} %dynamic_update_slice.3, f32[4096,2048]{1,0:T(8,128)} %multiply_add_fusion, pred[2048]{0:T(1024)(128)(4,1)S(1)} %get-tuple-element.14, pred[2048]{0:T(1024)(128)(4,1)S(1)} %get-tuple-element.13, pred[4096]{0:T(1024)(128)(4,1)S(1)} %get-tuple-element.12, ...), kind=kOutput, calls=%fused_computation | convolution fusion | flops 103121158144 | bytes 117452800 | tf_op jit(solution)/shard_map/dot_general | solution.py:92
  (42 shorter events, 19.0 us)
Async XLA Ops:
  6.5 1.6 copy-start
  6.5 89.7 %all-gather.11.cloned.1.call-start = ((), (), s32[]{:S(2)}) async-start(), calls=%async_computation | async-start | bytes 1310720 | tf_op jit(solution)/shard_map/all_gather | solution.py:53
  68.5 84.3 %all-gather.15.cloned.1.call-start = ((), (), s32[]{:S(2)}) async-start(), calls=%async_computation.2 | async-start | bytes 9437184 | tf_op jit(solution)/shard_map/all_gather | solution.py:10
  99.0 110.0 %all-gather.17.cloned.1.call-start = ((), (), s32[]{:S(2)}) async-start(), calls=%async_computation.3 | async-start | bytes 9437184 | tf_op jit(solution)/shard_map/all_gather | solution.py:10
  99.8 205.2 %all-gather.19.cloned.1.call-start = ((), (), s32[]{:S(2)}) async-start(), calls=%async_computation.4 | async-start | bytes 2621440 | tf_op jit(solution)/shard_map/all_gather | solution.py:10
  152.8 61.4 %copy-start.4 = (bf16[256,2048]{1,0:T(8,128)(2,1)S(1)}, bf16[256,2048]{1,0:T(8,128)(2,1)}, u32[]{:S(2)}) copy-start(bf16[256,2048]{1,0:T(8,128)(2,1)} %all-gather.11.cloned.1.call-done) | copy-start | bytes 3145732
  256.4 1.9 copy-start.2
  259.2 396.4 %all-gather.13.cloned.1.call-start = ((), (), s32[]{:S(2)}) async-start(), calls=%async_computation.1 | async-start | bytes 75497472 | tf_op jit(solution)/shard_map/all_gather | solution.py:10
  311.1 9.4 copy-start.5
  320.6 16.8 %copy-start.3 = (bf16[4096,512]{0,1:T(8,128)(2,1)S(1)}, bf16[4096,512]{0,1:T(8,128)(2,1)}, u32[]{:S(2)}) copy-start(bf16[4096,512]{0,1:T(8,128)(2,1)} %copy-done.2) | copy-start | bytes 12582916
  353.9 632.7 %all-gather.21.cloned.1.call-start = ((), (), s32[]{:S(2)}) async-start(), calls=%async_computation.5 | async-start | bytes 20971520 | tf_op jit(solution)/shard_map/all_gather | solution.py:10
  1003.9 123.6 %copy-start.1 = (bf16[1024,1024]{1,0:T(8,128)(2,1)S(1)}, bf16[1024,1024]{1,0:T(8,128)(2,1)}, u32[]{:S(2)}) copy-start(bf16[1024,1024]{1,0:T(8,128)(2,1)} %param.8) | copy-start | bytes 6291460
Sparse Core Ops, SparseCore 0:
  68.7 27.5 all-gather.10
  99.1 53.6 all-gather.14
  154.7 54.2 all-gather.16
  259.3 45.6 all-gather.18
  354.0 301.5 all-gather.12
  699.8 286.7 all-gather.20
